TPU v7x, 256 devices: a whole 4x4x8 slice. The times are simulated.
256 devices in a mesh: patch: 16 (over z_hi, x), wrow: 4 (over z_lo, core), wcol: 4 (over y).
Axes of the slice: x: 4, y: 4, z: 8 (z_hi: 4, z_lo: 2; z = z_hi * 2 + z_lo), core: 2. Of those that a mesh axis runs over, the one named last changes fastest.
Arguments:
- hidden_states: bfloat16 [4, 8192, 1536], P('wrow', ('patch', 'wcol')), may hold values from -6 to 6
- modulation: float32 [4, 3, 1536], P('wrow'), may hold values from -4 to 4
- w_qkv: bfloat16 [1536, 3, 1536], P('wrow', None, 'wcol'), may hold values from -1 to 1
- w_out: bfloat16 [1536, 1536], P('wcol', 'wrow'), may hold values from -0.15625 to 0.15625
- lengths: int32 [4], P('wrow'), may hold values from 1 to 8192, 20480 in all
Outputs:
- updated: bfloat16 [4, 8192, 1536], P('wrow', ('patch', 'wcol'))
Inputs may be any that keep to these rules, and one draw needn't show every extreme that they name: lengths[v] real tokens in video v, padding after them; the longest video fills all 8192 slots.
All inputs are finite; a program needn't handle non-finite values. No bound on the sum of `lengths` on one device may be relied on, other than what follows from the above.
Results may differ from a plain program's by a relative error of at most 0.015.
The roundings to bfloat16 on the way count: a program that leaves them out, or rounds other values in their place, can miss the bound.
Values may be sent and summed in bfloat16 or wider, within the bound.
A program may use at most 64 MiB of HBM per device.

v0:
```python
import jax
import jax.numpy as jnp
from jax import lax
from jax.sharding import PartitionSpec as P

HD = 128
EPSILON = 1e-06
FLOOR = -1e30


def modulated_norm(states, shift, scale):
    values = states.astype(jnp.float32)
    center = jnp.mean(values, axis=-1, keepdims=True)
    spread = jnp.mean(jnp.square(values - center), axis=-1, keepdims=True)
    return ((values - center) * lax.rsqrt(spread + EPSILON) * (1.0 + scale) + shift).astype(
        jnp.bfloat16
    )


def absorb(carry, keys, values, first, queries, limits):
    peak, weight_sum, numer = carry
    videos_here = keys.shape[0]
    count = keys.shape[1]
    heads_here = queries.shape[2]
    head_size = queries.shape[3]
    key_heads = keys.reshape(videos_here, count, heads_here, head_size)
    value_heads = values.reshape(videos_here, count, heads_here, head_size)
    scores = jnp.einsum(
        "vqhd,vkhd->vhqk", queries, key_heads, preferred_element_type=jnp.float32
    ) * head_size ** (-0.5)
    position = first + jnp.arange(count, dtype=jnp.int32)
    valid = (position[None, :] < limits[:, None])[:, None, None, :]
    scores = jnp.where(valid, scores, FLOOR)
    new_peak = jnp.maximum(peak, jnp.max(scores, axis=-1))
    factor = jnp.exp(peak - new_peak)
    probs = jnp.exp(scores - new_peak[..., None]) * valid.astype(jnp.float32)
    weight_sum = weight_sum * factor + jnp.sum(probs, axis=-1)
    numer = numer * factor[..., None] + jnp.einsum(
        "vhqk,vkhd->vhqd",
        probs.astype(jnp.bfloat16),
        value_heads,
        preferred_element_type=jnp.float32,
    )
    return (new_peak, weight_sum, numer)


def body(hidden_states, modulation, w_qkv, w_out, lengths):
    videos_here = hidden_states.shape[0]
    width = hidden_states.shape[2]
    shift = modulation[:, 0][:, None, :]
    scale = modulation[:, 1][:, None, :]
    gate = modulation[:, 2][:, None, :]
    normed = modulated_norm(hidden_states, shift, scale)
    tile_rows = lax.all_gather(normed, "wcol", axis=1, tiled=True)
    tile_len = tile_rows.shape[1]
    local_cols = w_qkv.shape[2]
    flat_rows = tile_rows.reshape(videos_here * tile_len, width)
    piece = lax.all_gather(w_qkv, "wrow", axis=0, tiled=True)
    mixed = jnp.dot(
        flat_rows, piece.reshape(piece.shape[0], 3 * local_cols), preferred_element_type=jnp.float32
    )
    mixed = mixed.reshape(videos_here, tile_len, 3 * local_cols)
    mixed = mixed.astype(jnp.bfloat16).reshape(videos_here, tile_len, 3, local_cols)
    heads_here = local_cols // HD
    queries = mixed[:, :, 0].reshape(videos_here, tile_len, heads_here, HD)
    keys = mixed[:, :, 1]
    values = mixed[:, :, 2]
    start_peak = jnp.full((videos_here, heads_here, tile_len), FLOOR, jnp.float32)
    start_sum = jnp.zeros((videos_here, heads_here, tile_len), jnp.float32)
    start_numer = jnp.zeros((videos_here, heads_here, tile_len, HD), jnp.float32)
    key_piece = lax.all_gather(keys, "patch", axis=1, tiled=True)
    value_piece = lax.all_gather(values, "patch", axis=1, tiled=True)
    count = key_piece.shape[1]
    block_len = 512

    def one_block(index, inner):
        offset = index * block_len
        key_block = lax.dynamic_slice_in_dim(key_piece, offset, block_len, 1)
        value_block = lax.dynamic_slice_in_dim(value_piece, offset, block_len, 1)
        return absorb(inner, key_block, value_block, offset, queries, lengths)

    peak, weight_sum, numer = lax.fori_loop(
        0, count // block_len, one_block, (start_peak, start_sum, start_numer)
    )
    attended = (numer / weight_sum[..., None]).astype(jnp.bfloat16)
    attended = jnp.transpose(attended, (0, 2, 1, 3)).reshape(videos_here * tile_len, local_cols)
    partial_out = jnp.dot(
        attended,
        lax.all_gather(w_out, "wrow", axis=1, tiled=True),
        preferred_element_type=jnp.float32,
    )
    partial_out = partial_out.reshape(videos_here, tile_len, width)
    out_proj = lax.psum_scatter(
        partial_out.astype(jnp.bfloat16), "wcol", scatter_dimension=1, tiled=True
    ).astype(jnp.float32)
    return (hidden_states.astype(jnp.float32) + gate * out_proj).astype(jnp.bfloat16)


def solution(mesh):
    placed = (
        P("wrow", ("patch", "wcol"), None),
        P("wrow", None, None),
        P("wrow", None, "wcol"),
        P("wcol", "wrow"),
        P("wrow"),
    )
    return jax.shard_map(
        body,
        mesh=mesh,
        in_specs=placed,
        out_specs=P("wrow", ("patch", "wcol"), None),
        check_vma=False,
    )
```

profile of v0, /device:TPU:2, one launch (start us, length us, event | category | flops | bytes accessed | tf_op | source)
XLA Modules:
  0.0 490.6 jit_solution(7066353537932086624)
XLA Ops:
  6.5 1.4 slice_reduce_fusion.1
  7.9 1.1 convert_reduce_fusion
  9.0 1.2 fusion.21
  10.3 2.1 fusion.24
  12.4 2.3 copy.12
  14.8 29.8 %all-gather.8.cloned.1.call-done = bf16[1,512,1536]{2,1,0:T(8,128)(2,1)} async-done(((bf16[1,128,1536]{2,1,0:T(8,128)(2,1)}), bf16[1,512,1536]{2,1,0:T(8,128)(2,1)}) %all-gather.8.cloned.1.call-update) | async-done | bytes 1572880 | tf_op jit(solution)/shard_map/all_gather | solution.py:54
  44.6 45.2 %all-gather.10.cloned.1.call-done = bf16[1536,3,384]{0,2,1:T(8,128)(2,1)} async-done(((bf16[384,3,384]{0,2,1:T(8,128)(2,1)}), bf16[1536,3,384]{0,2,1:T(8,128)(2,1)}) %all-gather.10.cloned.1.call-update) | async-done | bytes 3538960 | tf_op jit(solution)/shard_map/all_gather | solution.py:58
  89.8 4.7 convolution_convert_fusion
  95.2 1.0 fusion.27
  97.7 103.0 %all-gather.14.cloned.1.call-done = bf16[1,8192,1,384]{1,3,2,0:T(8,128)(2,1)} async-done(((bf16[1,512,1,384]{1,3,2,0:T(8,128)(2,1)}), bf16[1,8192,1,384]{1,3,2,0:T(8,128)(2,1)}) %all-gather.14.cloned.1.call-update) | async-done | bytes 6291472 | tf_op jit(solution)/shard_map/all_gather | solution.py:71
  200.7 104.5 %all-gather.16.cloned.1.call-done = bf16[1,8192,1,384]{1,3,2,0:T(8,128)(2,1)} async-done(((bf16[1,512,1,384]{1,3,2,0:T(8,128)(2,1)}), bf16[1,8192,1,384]{1,3,2,0:T(8,128)(2,1)}) %all-gather.16.cloned.1.call-update) | async-done | bytes 6291472 | tf_op jit(solution)/shard_map/all_gather | solution.py:72
  305.2 143.9 %while.18 = (s32[]{:T(128)}, f32[1,3,512]{2,1,0:T(4,128)S(1)}, f32[1,3,512]{2,1,0:T(4,128)}, f32[1,3,512,128]{3,2,1,0:T(8,128)}, s32[1]{0:T(128)}, /*index=5*/bf...) while((s32[]{:T(128)}, f32[1,3,512]{2,1,0:T(4,128)S(1)}, ...), condition=%wide.region_5.6_spmd.clone, body=%wide.region_2.5_spmd.clone.sunk | while | flops 413477376 | bytes 13930823 | solution.py:82
  305.2 1.9 constant_dynamic-slice_fusion.3
  307.2 1.2 fusion.43
  309.3 3.2 fusion.46
  314.0 1.9 constant_dynamic-slice_fusion.3
  315.9 1.2 fusion.43
  318.0 3.5 fusion.46
  323.0 1.9 constant_dynamic-slice_fusion.3
  325.0 1.2 fusion.43
  327.1 3.4 fusion.46
  332.0 1.9 constant_dynamic-slice_fusion.3
  334.0 1.2 fusion.43
  336.1 3.4 fusion.46
  341.1 1.9 constant_dynamic-slice_fusion.3
  343.0 1.2 fusion.43
  345.1 3.4 fusion.46
  350.1 1.9 constant_dynamic-slice_fusion.3
  352.0 1.2 fusion.43
  354.1 3.4 fusion.46
  359.1 1.9 constant_dynamic-slice_fusion.3
  361.0 1.2 fusion.43
  363.1 3.4 fusion.46
  368.1 1.9 constant_dynamic-slice_fusion.3
  370.0 1.2 fusion.43
  372.1 3.4 fusion.46
  377.1 1.9 constant_dynamic-slice_fusion.3
  379.0 1.2 fusion.43
  381.1 3.4 fusion.46
  386.1 1.9 constant_dynamic-slice_fusion.3
  388.0 1.2 fusion.43
  390.1 3.4 fusion.46
  395.1 1.9 constant_dynamic-slice_fusion.3
  397.0 1.2 fusion.43
  399.2 3.4 fusion.46
  404.1 1.9 constant_dynamic-slice_fusion.3
  406.0 1.2 fusion.43
  408.2 3.4 fusion.46
  413.1 1.9 constant_dynamic-slice_fusion.3
  415.1 1.2 fusion.43
  417.2 3.4 fusion.46
  422.2 1.9 constant_dynamic-slice_fusion.3
  424.1 1.2 fusion.43
  426.2 3.4 fusion.46
  431.2 1.9 constant_dynamic-slice_fusion.3
  433.1 1.2 fusion.43
  435.2 3.4 fusion.46
  440.2 1.9 constant_dynamic-slice_fusion.3
  442.1 1.2 fusion.43
  444.2 3.4 fusion.46
  449.2 1.4 copy.15
  451.5 3.4 fusion.17
  454.9 27.0 %reduce-scatter.2.cloned.1.call-done = bf16[1,128,1536]{2,1,0:T(8,128)(2,1)} async-done(((bf16[1,512,1536]{2,1,0:T(8,128)(2,1)}), bf16[1,128,1536]{2,1,0:T(8,128)(2,1)}) %reduce-scatter.2.cloned.1.call-update) | async-done | bytes 393232 | tf_op jit(solution)/shard_map/reduce_scatter | solution.py:93
  481.9 1.9 fusion.25
  (265 shorter events, 40.2 us)
Async XLA Ops:
  6.5 38.1 %all-gather.8.cloned.1.call-start = ((), (), s32[]{:S(2)}) async-start(), calls=%async_computation.1 | async-start | bytes 1966080 | tf_op jit(solution)/shard_map/all_gather | solution.py:54
  12.4 77.4 %all-gather.10.cloned.1.call-start = ((), (), s32[]{:S(2)}) async-start(), calls=%async_computation.2 | async-start | bytes 4423680 | tf_op jit(solution)/shard_map/all_gather | solution.py:58
  14.7 186.0 %all-gather.14.cloned.1.call-start = ((), (), s32[]{:S(2)}) async-start(), calls=%async_computation.5 | async-start | bytes 6684672 | tf_op jit(solution)/shard_map/all_gather | solution.py:71
  96.2 209.0 %all-gather.16.cloned.1.call-start = ((), (), s32[]{:S(2)}) async-start(), calls=%async_computation.6 | async-start | bytes 6684672 | tf_op jit(solution)/shard_map/all_gather | solution.py:72
  96.8 354.7 %all-gather.12.cloned.1.call-start = ((), (), s32[]{:S(2)}) async-start(), calls=%async_computation.3 | async-start | bytes 1474560 | tf_op jit(solution)/shard_map/all_gather | solution.py:89
  97.4 384.6 %reduce-scatter.2.cloned.1.call-start = ((), (), s32[]{:S(2)}) async-start(), calls=%async_computation.4 | async-start | bytes 1966080 | tf_op jit(solution)/shard_map/reduce_scatter | solution.py:93
  309.2 3.2 copy-start.3
  309.3 3.2 copy-start.5
  312.5 0.9 copy-start.1
  317.1 0.8 copy-start.4
  318.0 3.5 copy-start.3
  318.0 3.5 copy-start.5
  321.5 0.9 copy-start.1
  327.0 3.5 copy-start.3
  327.1 3.5 copy-start.5
  330.5 0.9 copy-start.1
  335.2 0.8 copy-start.4
  336.1 3.5 copy-start.3
  336.1 3.5 copy-start.5
  339.5 0.9 copy-start.1
  344.2 0.8 copy-start.4
  345.1 3.5 copy-start.3
  345.1 3.5 copy-start.5
  348.5 0.9 copy-start.1
  353.2 0.8 copy-start.4
  354.1 3.5 copy-start.3
  354.1 3.5 copy-start.5
  357.6 0.9 copy-start.1
  362.2 0.8 copy-start.4
  363.1 3.5 copy-start.3
  363.1 3.5 copy-start.5
  366.6 0.9 copy-start.1
  371.2 0.8 copy-start.4
  372.1 3.5 copy-start.3
  372.1 3.5 copy-start.5
  375.6 0.9 copy-start.1
  381.1 3.5 copy-start.3
  381.1 3.5 copy-start.5
  384.6 0.9 copy-start.1
  389.3 0.8 copy-start.4
  390.1 3.5 copy-start.3
  390.1 3.5 copy-start.5
  393.6 0.9 copy-start.1
  399.1 3.5 copy-start.3
  399.1 3.5 copy-start.5
  402.6 0.9 copy-start.1
  408.1 3.5 copy-start.3
  408.2 3.5 copy-start.5
  411.6 0.9 copy-start.1
  417.2 3.5 copy-start.3
  417.2 3.5 copy-start.5
  420.6 0.9 copy-start.1
  425.3 0.8 copy-start.4
  426.2 3.5 copy-start.3
  426.2 3.5 copy-start.5
  429.6 0.9 copy-start.1
  435.2 3.5 copy-start.3
  435.2 3.5 copy-start.5
  438.6 0.9 copy-start.1
  444.2 3.5 copy-start.3
  444.2 3.5 copy-start.5
  447.7 0.9 copy-start.1
  450.6 31.3 %copy-start = (bf16[1,128,1536]{2,1,0:T(8,128)(2,1)S(1)}, bf16[1,128,1536]{2,1,0:T(8,128)(2,1)}, u32[]{:S(2)}) copy-start(bf16[1,128,1536]{2,1,0:T(8,128)(2,1)} %param.7) | copy-start | bytes 1179652
  450.6 31.3 %copy-start.6 = (f32[1536]{0:T(1024)S(1)}, f32[1536]{0:T(1024)}, u32[]{:S(2)}) copy-start(f32[1536]{0:T(1024)} %get-tuple-element.182) | copy-start | bytes 18436
  (24 other events, 16.1 us)
Sparse Core Ops, SparseCore 0:
  12.5 32.0 all-gather.7
  46.4 43.3 all-gather.9
  96.3 104.3 all-gather.13
  203.0 102.2 all-gather.15
  306.9 22.7 all-gather.11
  455.0 26.8 reduce-scatter.1
where the time goes:
time: 492 us; the launch traced here: 491 us
  waiting for transfers between devices  311 us (63%)
  matrix products  76 us (15%)
  local copies, waits for them, and re-layouts  45.7 us (9%)
  other arithmetic  43.1 us (9%)
  between operations  13.6 us (3%)
    all_gather x1, waiting for transfers between devices, body(): value_piece = lax.all_gather(values, 'patch', axis=1, tiled=True)  105 us
    all_gather x1, waiting for transfers between devices, body(): key_piece = lax.all_gather(keys, 'patch', axis=1, tiled=True)  103 us
    dot_general x16, matrix products, absorb(): jnp.einsum('vhqk,vkhd->vhqd', probs.astype(jnp.bfloat16), value_heads, pr...  54.9 us
    all_gather x1, waiting for transfers between devices, body(): piece = lax.all_gather(w_qkv, 'wrow', axis=0, tiled=True)  45.2 us
    dynamic_slice x16, local copies, waits for them, and re-layouts, one_block(): value_block = lax.dynamic_slice_in_dim(value_piece, offset, block_len, 1)  30.6 us
    all_gather x1, waiting for transfers between devices, body(): tile_rows = lax.all_gather(normed, 'wcol', axis=1, tiled=True)  29.8 us
    reduce_scatter x1, waiting for transfers between devices, body(): lax.psum_scatter(partial_out.astype(jnp.bfloat16), 'wcol', scatter_dimens...  27 us
    convert_element_type x16, other arithmetic, absorb(): probs = jnp.exp(scores - new_peak[..., None]) * valid.astype(jnp.float32)  19.9 us
  transfers between devices with their start and end apart: 6, of which 5 were waited for; matrix products, arithmetic and copies ran while one was open for 28% of the time, Pallas kernels for 0%

commit v1 on v0

--- a/solution.py
+++ b/solution.py
@@ -1,3 +1,4 @@
+import functools
 import jax
 import jax.numpy as jnp
 from jax import lax
@@ -6,6 +7,22 @@
 HD = 128
 EPSILON = 1e-06
 FLOOR = -1e30
+
+
+def draft_table_in(u, axis_tag):
+    n_chips = lax.axis_size(axis_tag)
+    part_next = list(map(lambda t: (t - 1, t), range(1, n_chips)))
+    x_new = part_next + [(n_chips - 1, 0)]
+    e_now = u
+    found = [e_now]
+    for _ in range(n_chips - 1):
+        e_now = lax.ppermute(e_now, axis_tag, x_new)
+        found += [e_now]
+    y1 = jnp.concatenate([*reversed(found)], axis=1)
+    return jnp.roll(y1, (lax.axis_index(axis_tag) + 1) * e_now.shape[1], axis=1)
+
+
+set_note = functools.partial(draft_table_in, axis_tag="wcol")
 
 
 def modulated_norm(states, shift, scale):
@@ -51,7 +68,7 @@
     scale = modulation[:, 1][:, None, :]
     gate = modulation[:, 2][:, None, :]
     normed = modulated_norm(hidden_states, shift, scale)
-    tile_rows = lax.all_gather(normed, "wcol", axis=1, tiled=True)
+    tile_rows = set_note(normed)
     tile_len = tile_rows.shape[1]
     local_cols = w_qkv.shape[2]
     flat_rows = tile_rows.reshape(videos_here * tile_len, width)

time: 492 us -> 456 us (0.927)
  waiting for transfers between devices: 311 us -> 270 us
    all_gather x1, waiting for transfers between devices: 45.2 us -> 2.84 us  [body(): piece = lax.all_gather(w_qkv, 'wrow', axis=0, tiled=True)]
    ppermute x0 -> x3, waiting for transfers between devices: none -> 31.9 us  [draft_table_in(): e_now = lax.ppermute(e_now, axis_tag, x_new)]
    all_gather x1 -> x0, waiting for transfers between devices: 29.8 us -> none  [body(): tile_rows = lax.all_gather(normed, 'wcol', axis=1, tiled=True)]
  transfers between devices with their start and end apart: 6 -> 8, of which waited for: 5 -> 7; matrix products, arithmetic and copies ran while one was open for 28% -> 32% of each run, Pallas kernels for 0% -> 0%
where the time goes in v1:
time: 456 us; the launch traced here: 455 us
  waiting for transfers between devices  270 us (59%)
  matrix products  76.1 us (17%)
  local copies, waits for them, and re-layouts  50.4 us (11%)
  other arithmetic  41.4 us (9%)
  between operations  13.2 us (3%)
    all_gather x1, waiting for transfers between devices, body(): value_piece = lax.all_gather(values, 'patch', axis=1, tiled=True)  105 us
    all_gather x1, waiting for transfers between devices, body(): key_piece = lax.all_gather(keys, 'patch', axis=1, tiled=True)  103 us
    dot_general x16, matrix products, absorb(): jnp.einsum('vhqk,vkhd->vhqd', probs.astype(jnp.bfloat16), value_heads, pr...  55 us
    ppermute x3, waiting for transfers between devices, draft_table_in(): e_now = lax.ppermute(e_now, axis_tag, x_new)  31.9 us
    dynamic_slice x16, local copies, waits for them, and re-layouts, one_block(): value_block = lax.dynamic_slice_in_dim(value_piece, offset, block_len, 1)  30.6 us
    reduce_scatter x1, waiting for transfers between devices, body(): lax.psum_scatter(partial_out.astype(jnp.bfloat16), 'wcol', scatter_dimens...  26.9 us
    convert_element_type x16, other arithmetic, absorb(): probs = jnp.exp(scores - new_peak[..., None]) * valid.astype(jnp.float32)  18.8 us
    reduce_sum x16, other arithmetic, absorb(): weight_sum = weight_sum * factor + jnp.sum(probs, axis=-1)  14.2 us
  transfers between devices with their start and end apart: 8, of which 7 were waited for; matrix products, arithmetic and copies ran while one was open for 32% of the time, Pallas kernels for 0%

profile of v1, /device:TPU:2, one launch (start us, length us, event | category | flops | bytes accessed | tf_op | source)
XLA Modules:
  0.0 455.1 jit_solution(9167025986205443837)
XLA Ops:
  6.5 2.3 copy.12
  8.9 1.4 slice_reduce_fusion.1
  10.3 1.1 convert_reduce_fusion
  12.0 1.7 collective-permute-start
  13.7 10.6 %collective-permute-done = bf16[1,128,1536]{2,1,0:T(8,128)(2,1)S(1)} collective-permute-done((bf16[1,128,1536]{2,1,0:T(8,128)(2,1)S(1)}, bf16[1,128,1536]{2,1,0:T(8,128)(2,1)S(1)}, u32[]{:S(2)}, u32[]{:S(2)}) %collective-permute-start) | collective-permute-done | bytes 393248 | tf_op jit(solution)/shard_map/ppermute | solution.py:19
  24.5 11.0 %collective-permute-done.1 = bf16[1,128,1536]{2,1,0:T(8,128)(2,1)S(1)} collective-permute-done((bf16[1,128,1536]{2,1,0:T(8,128)(2,1)S(1)}, bf16[1,128,1536]{2,1,0:T(8,128)(2,1)S(1)}, u32[]{:S(2)}, u32[]{:S(2)}) %collective-permute-start.1) | collective-permute-done | bytes 393248 | tf_op jit(solution)/shard_map/ppermute | solution.py:19
  35.5 10.3 %collective-permute-done.2 = bf16[1,128,1536]{2,1,0:T(8,128)(2,1)S(1)} collective-permute-done((bf16[1,128,1536]{2,1,0:T(8,128)(2,1)S(1)}, bf16[1,128,1536]{2,1,0:T(8,128)(2,1)S(1)}, u32[]{:S(2)}, u32[]{:S(2)}) %collective-permute-start.2) | collective-permute-done | bytes 393248 | tf_op jit(solution)/shard_map/ppermute | solution.py:19
  52.6 2.8 all-gather.7.cloned.1.call-done
  55.5 4.7 %convolution_convert_fusion = bf16[512,1152]{1,0:T(8,128)(2,1)S(1)} fusion(bf16[1536,1152]{0,1:T(8,128)(2,1)} %bitcast.91, bf16[1,1024,1536]{2,1,0:T(8,128)(2,1)} %constant_dynamic-update-slice_fusion, s32[]{:T(128)S(6)} %select_n.34), kind=kOutput, calls=%fused_computation.23 | convolution fusion | flops 1812529152 | bytes 6291460 | tf_op jit(solution)/shard_map/dot_general | solution.py:76
  63.4 102.9 %all-gather.11.cloned.1.call-done = bf16[1,8192,1,384]{1,3,2,0:T(8,128)(2,1)} async-done(((bf16[1,512,1,384]{1,3,2,0:T(8,128)(2,1)}), bf16[1,8192,1,384]{1,3,2,0:T(8,128)(2,1)}) %all-gather.11.cloned.1.call-update) | async-done | bytes 6291472 | tf_op jit(solution)/shard_map/all_gather | solution.py:88
  166.3 104.7 %all-gather.13.cloned.1.call-done = bf16[1,8192,1,384]{1,3,2,0:T(8,128)(2,1)} async-done(((bf16[1,512,1,384]{1,3,2,0:T(8,128)(2,1)}), bf16[1,8192,1,384]{1,3,2,0:T(8,128)(2,1)}) %all-gather.13.cloned.1.call-update) | async-done | bytes 6291472 | tf_op jit(solution)/shard_map/all_gather | solution.py:89
  271.0 143.1 %while.18 = (s32[]{:T(128)}, f32[1,3,512]{2,1,0:T(4,128)S(1)}, f32[1,3,512]{2,1,0:T(4,128)}, f32[1,3,512,128]{3,2,1,0:T(8,128)}, s32[1]{0:T(128)}, /*index=5*/bf...) while((s32[]{:T(128)}, f32[1,3,512]{2,1,0:T(4,128)S(1)}, ...), condition=%wide.region_5.6_spmd.clone, body=%wide.region_2.5_spmd.clone.sunk | while | flops 413477376 | bytes 13930823 | solution.py:99
  271.0 1.9 constant_dynamic-slice_fusion.3
  272.9 1.2 fusion.45
  275.0 3.2 fusion.48
  279.7 1.9 constant_dynamic-slice_fusion.3
  281.6 1.2 fusion.45
  283.7 3.5 fusion.48
  288.7 1.9 constant_dynamic-slice_fusion.3
  290.7 1.2 fusion.45
  292.7 3.4 fusion.48
  297.7 1.9 constant_dynamic-slice_fusion.3
  299.6 1.2 fusion.45
  301.7 3.4 fusion.48
  306.7 1.9 constant_dynamic-slice_fusion.3
  308.6 1.2 fusion.45
  310.6 3.4 fusion.48
  315.6 1.9 constant_dynamic-slice_fusion.3
  317.5 1.2 fusion.45
  319.6 3.4 fusion.48
  324.6 1.9 constant_dynamic-slice_fusion.3
  326.5 1.2 fusion.45
  328.5 3.4 fusion.48
  333.5 1.9 constant_dynamic-slice_fusion.3
  335.4 1.2 fusion.45
  337.5 3.4 fusion.48
  342.5 1.9 constant_dynamic-slice_fusion.3
  344.4 1.2 fusion.45
  346.4 3.4 fusion.48
  351.4 1.9 constant_dynamic-slice_fusion.3
  353.3 1.2 fusion.45
  355.4 3.4 fusion.48
  360.4 1.9 constant_dynamic-slice_fusion.3
  362.3 1.2 fusion.45
  364.3 3.4 fusion.48
  369.3 1.9 constant_dynamic-slice_fusion.3
  371.2 1.2 fusion.45
  373.3 3.4 fusion.48
  378.3 1.9 constant_dynamic-slice_fusion.3
  380.2 1.2 fusion.45
  382.2 3.4 fusion.48
  387.2 1.9 constant_dynamic-slice_fusion.3
  389.1 1.2 fusion.45
  391.2 3.4 fusion.48
  396.2 1.9 constant_dynamic-slice_fusion.3
  398.1 1.2 fusion.45
  400.1 3.4 fusion.48
  405.1 1.9 constant_dynamic-slice_fusion.3
  407.0 1.2 fusion.45
  409.1 3.4 fusion.48
  414.1 1.4 copy.15
  416.4 3.4 fusion.17
  419.8 26.9 %reduce-scatter.2.cloned.1.call-done = bf16[1,128,1536]{2,1,0:T(8,128)(2,1)} async-done(((bf16[1,512,1536]{2,1,0:T(8,128)(2,1)}), bf16[1,128,1536]{2,1,0:T(8,128)(2,1)}) %reduce-scatter.2.cloned.1.call-update) | async-done | bytes 393232 | tf_op jit(solution)/shard_map/reduce_scatter | solution.py:110
  446.7 1.9 fusion.26
  (278 shorter events, 49.0 us)
Async XLA Ops:
  6.5 4.9 %copy-start = (bf16[1,128,1536]{2,1,0:T(8,128)(2,1)S(1)}, bf16[1,128,1536]{2,1,0:T(8,128)(2,1)}, u32[]{:S(2)}) copy-start(bf16[1,128,1536]{2,1,0:T(8,128)(2,1)} %param.7) | copy-start | bytes 1179652
  6.5 48.9 %all-gather.7.cloned.1.call-start = ((), (), s32[]{:S(2)}) async-start(), calls=%async_computation.1 | async-start | bytes 4423680 | tf_op jit(solution)/shard_map/all_gather | solution.py:75
  8.9 157.5 %all-gather.11.cloned.1.call-start = ((), (), s32[]{:S(2)}) async-start(), calls=%async_computation.4 | async-start | bytes 6684672 | tf_op jit(solution)/shard_map/all_gather | solution.py:88
  12.0 12.2 %collective-permute-start = (bf16[1,128,1536]{2,1,0:T(8,128)(2,1)S(1)}, bf16[1,128,1536]{2,1,0:T(8,128)(2,1)S(1)}, u32[]{:S(2)}, u32[]{:S(2)}) collective-permute-start(bf16[1,128,1536]{2,1,0:T(8,128)(2,1)S(1)} %fusion.25), channel_id=1, source_target_pairs={{0,1},{1,2},{2,3},{3,0},{4,5},{5,6},{6,7},{7,4},{8,9},{9,10},{10,1... | collective-permute-start | bytes 1179656 | tf_op jit(solution)/shard_map/ppermute | solution.py:19
  24.2 11.3 %collective-permute-start.1 = (bf16[1,128,1536]{2,1,0:T(8,128)(2,1)S(1)}, bf16[1,128,1536]{2,1,0:T(8,128)(2,1)S(1)}, u32[]{:S(2)}, u32[]{:S(2)}) collective-permute-start(bf16[1,128,1536]{2,1,0:T(8,128)(2,1)S(1)} %collective-permute-done), channel_id=1, source_target_pairs={{0,1},{1,2},{2,3},{3,0},{4,5},{5,6},{6,7},{7,4},{8,9},{9,10},{10,1... | collective-permute-start | bytes 1179656 | tf_op jit(solution)/shard_map/ppermute | solution.py:19
  35.5 10.3 %collective-permute-start.2 = (bf16[1,128,1536]{2,1,0:T(8,128)(2,1)S(1)}, bf16[1,128,1536]{2,1,0:T(8,128)(2,1)S(1)}, u32[]{:S(2)}, u32[]{:S(2)}) collective-permute-start(bf16[1,128,1536]{2,1,0:T(8,128)(2,1)S(1)} %collective-permute-done.1), channel_id=1, source_target_pairs={{0,1},{1,2},{2,3},{3,0},{4,5},{5,6},{6,7},{7,4},{8,9},{9,10},{10,1... | collective-permute-start | bytes 1179656 | tf_op jit(solution)/shard_map/ppermute | solution.py:19
  61.8 209.2 %all-gather.13.cloned.1.call-start = ((), (), s32[]{:S(2)}) async-start(), calls=%async_computation.5 | async-start | bytes 6684672 | tf_op jit(solution)/shard_map/all_gather | solution.py:89
  62.6 353.8 %all-gather.9.cloned.1.call-start = ((), (), s32[]{:S(2)}) async-start(), calls=%async_computation.2 | async-start | bytes 1474560 | tf_op jit(solution)/shard_map/all_gather | solution.py:106
  63.1 383.6 %reduce-scatter.2.cloned.1.call-start = ((), (), s32[]{:S(2)}) async-start(), calls=%async_computation.3 | async-start | bytes 1966080 | tf_op jit(solution)/shard_map/reduce_scatter | solution.py:110
  275.0 3.2 copy-start.4
  275.0 3.2 copy-start.6
  278.2 0.9 copy-start.2
  283.7 3.6 copy-start.4
  283.7 3.6 copy-start.6
  287.2 0.9 copy-start.2
  292.7 3.5 copy-start.4
  292.7 3.5 copy-start.6
  296.2 0.9 copy-start.2
  301.6 3.5 copy-start.4
  301.7 3.5 copy-start.6
  305.1 0.9 copy-start.2
  310.6 3.5 copy-start.4
  310.6 3.5 copy-start.6
  314.1 0.9 copy-start.2
  318.7 0.8 copy-start.5
  319.6 3.5 copy-start.4
  319.6 3.5 copy-start.6
  323.0 0.9 copy-start.2
  327.7 0.8 copy-start.5
  328.5 3.5 copy-start.4
  328.5 3.5 copy-start.6
  332.0 0.9 copy-start.2
  336.6 0.8 copy-start.5
  337.5 3.5 copy-start.4
  337.5 3.5 copy-start.6
  340.9 0.9 copy-start.2
  345.6 0.8 copy-start.5
  346.4 3.5 copy-start.4
  346.4 3.5 copy-start.6
  349.9 0.9 copy-start.2
  354.5 0.8 copy-start.5
  355.4 3.5 copy-start.4
  355.4 3.5 copy-start.6
  358.8 0.9 copy-start.2
  364.3 3.5 copy-start.4
  364.3 3.5 copy-start.6
  367.8 0.9 copy-start.2
  373.3 3.5 copy-start.4
  373.3 3.5 copy-start.6
  376.7 0.9 copy-start.2
  382.2 3.5 copy-start.4
  382.2 3.5 copy-start.6
  385.7 0.9 copy-start.2
  391.2 3.5 copy-start.4
  391.2 3.5 copy-start.6
  394.6 0.9 copy-start.2
  400.1 3.5 copy-start.4
  400.1 3.5 copy-start.6
  403.6 0.9 copy-start.2
  409.1 3.5 copy-start.4
  409.1 3.5 copy-start.6
  412.5 0.9 copy-start.2
  415.5 31.3 %copy-start.1 = (bf16[1,128,1536]{2,1,0:T(8,128)(2,1)S(1)}, bf16[1,128,1536]{2,1,0:T(8,128)(2,1)}, u32[]{:S(2)}) copy-start(bf16[1,128,1536]{2,1,0:T(8,128)(2,1)} %param.7) | copy-start | bytes 1179652
  415.5 31.3 %copy-start.7 = (f32[1536]{0:T(1024)S(1)}, f32[1536]{0:T(1024)}, u32[]{:S(2)}) copy-start(f32[1536]{0:T(1024)} %get-tuple-element.182) | copy-start | bytes 18436
  (27 other events, 18.6 us)
Sparse Core Ops, SparseCore 0:
  9.2 46.2 all-gather.6
  61.9 104.3 all-gather.10
  168.7 102.2 all-gather.12
  272.7 22.7 all-gather.8
  419.9 26.7 reduce-scatter.1
